TPU v7x, 32 devices: a whole 2x2x4 slice. The times are simulated.
32 devices in a mesh: pb: 4 (over y, core), wa: 8 (over z, x).
Axes of the slice: x: 2, y: 2, z: 4, core: 2. Of those that a mesh axis runs over, the one named last changes fastest.
Arguments:
- state: float32 [2, 8388608], P(None, ('pb', 'wa')), may hold values from -6 to 6
- gate_bank: float32 [4, 2, 128, 128], replicated, may hold values from -0.375 to 0.375
- pass_order: int32 [4], replicated, may hold values from 0 to 3, each once
Outputs:
- evolved: float32 [2, 8388608], P(None, ('pb', 'wa'))
Inputs may be any that keep to these rules, and one draw needn't show every extreme that they name: `pass_order`: each pass index 0 to 3 appears once.
All inputs are finite; a program needn't handle non-finite values.
Results may differ from a plain program's by a relative error of at most 0.0001.
Values sent between devices are 32-bit elements; how exact they have to be, the bound alone decides.
A program may use at most 64 MiB of HBM per device.

v0:
```python
import jax
import jax.numpy as jnp
from jax import lax
from jax.sharding import PartitionSpec as P

HIGH = lax.Precision.HIGHEST


def mix_left(gate, values):
    real = jnp.dot(gate[0], values[0], precision=HIGH) - jnp.dot(gate[1], values[1], precision=HIGH)
    imag = jnp.dot(gate[0], values[1], precision=HIGH) + jnp.dot(gate[1], values[0], precision=HIGH)
    return jnp.stack([real, imag])


def mix_right(gate, values):
    real = jnp.dot(values[0], gate[0].T, precision=HIGH) - jnp.dot(
        values[1], gate[1].T, precision=HIGH
    )
    imag = jnp.dot(values[1], gate[0].T, precision=HIGH) + jnp.dot(
        values[0], gate[1].T, precision=HIGH
    )
    return jnp.stack([real, imag])


def select_gate(gate_bank, pass_order, which):
    picked = pass_order[which] == jnp.arange(gate_bank.shape[0], dtype=jnp.int32)
    return jnp.sum(jnp.where(picked[:, None, None, None], gate_bank, 0.0), axis=0)


def trade_global(packed):
    return lax.all_to_all(
        lax.all_to_all(packed, "pb", split_axis=1, concat_axis=1, tiled=True),
        "wa",
        split_axis=2,
        concat_axis=2,
        tiled=True,
    )


def pack_block(block, groups, wa_count, middle):
    shaped = block.reshape(2, groups, 2, middle, wa_count // 2, -1)
    moved = jnp.transpose(shaped, (0, 1, 2, 4, 3, 5))
    return moved.reshape(2, groups, wa_count, middle, -1)


def unpack_block(packed, groups, wa_count, middle):
    shaped = packed.reshape(2, groups, 2, wa_count // 2, middle, -1)
    return jnp.transpose(shaped, (0, 1, 2, 4, 3, 5)).reshape(2, -1)


def per_device(state, gate_bank, pass_order):
    groups = lax.axis_size("pb")
    wa_count = lax.axis_size("wa")
    gate_rows = gate_bank.shape[2]
    middle = gate_rows // (2 * groups)
    psi = state
    first = select_gate(gate_bank, pass_order, 0)
    psi = mix_right(first, psi.reshape(2, -1, gate_rows)).reshape(2, -1)
    packed = trade_global(pack_block(psi, groups, wa_count, middle))
    second = select_gate(gate_bank, pass_order, 1)
    shaped = packed.reshape(2, groups, 2, wa_count // 2, middle, -1)
    moved = jnp.transpose(shaped, (0, 1, 2, 4, 3, 5))
    moved_shape = moved.shape
    mixed = mix_left(second, moved.reshape(2, gate_rows, -1)).reshape(moved_shape)
    psi = jnp.transpose(mixed, (0, 1, 2, 4, 3, 5)).reshape(2, -1)
    third = select_gate(gate_bank, pass_order, 2)
    psi = mix_right(third, psi.reshape(2, -1, gate_rows)).reshape(2, -1)
    fourth = select_gate(gate_bank, pass_order, 3)
    shaped = psi.reshape(2, groups, wa_count // 2, 2, middle, -1)
    moved = jnp.transpose(shaped, (0, 1, 3, 4, 2, 5))
    moved_shape = moved.shape
    mixed = mix_left(fourth, moved.reshape(2, gate_rows, -1)).reshape(moved_shape)
    packed = jnp.transpose(mixed, (0, 1, 4, 2, 3, 5)).reshape(2, groups, wa_count, middle, -1)
    psi = unpack_block(trade_global(packed), groups, wa_count, middle)
    return psi


def solution(mesh):
    in_specs = (P(None, ("pb", "wa")), P(), P())
    out_specs = P(None, ("pb", "wa"))
    return jax.shard_map(
        per_device, mesh=mesh, in_specs=in_specs, out_specs=out_specs, check_vma=False
    )
```

profile of v0, /device:TPU:0, one launch (start us, length us, event | category | flops | bytes accessed | tf_op | source)
XLA Modules:
  0.0 210.9 jit_solution(14688105302782742132)
XLA Ops:
  0.0 1.5 fusion.14
  1.5 4.3 %fusion.13 = (f32[1,262144]{1,0:T(1,128)S(1)}, f32[1,262144]{1,0:T(1,128)S(1)}) fusion(f32[2,262144]{1,0:T(2,128)} %param.3), kind=kLoop, calls=%fused_computation.42 | loop fusion | bytes 4194304 | tf_op jit(solution)/shard_map/slice | solution.py:16
  5.7 1.3 iota_compare_fusion
  7.0 1.2 iota_compare_fusion.2
  8.5 1.0 fusion.6
  9.5 1.0 fusion.7
  10.5 1.0 fusion
  11.6 1.0 fusion.1
  12.6 0.3 copy.25
  12.9 1.3 stack.36
  14.6 0.4 stack.37
  15.0 0.5 copy-done
  15.5 0.5 maximum_bitcast_fusion
  16.0 0.7 copy.41
  16.7 29.7 %all_to_all.20 = f32[2,4,8,16,512]{4,3,2,0,1:T(8,128)S(1)} all-to-all(f32[2,4,8,16,512]{4,3,2,0,1:T(8,128)S(1)} %bitcast.106), channel_id=1, replica_groups=mesh['pb'=4,'wa'=8] {'pb'}, dimensions={1} | all-to-all | bytes 4194304 | tf_op jit(solution)/shard_map/all_to_all | solution.py:32
  46.7 53.6 %all_to_all.21 = f32[2,4,8,16,512]{4,3,1,0,2:T(8,128)S(1)} all-to-all(f32[2,4,8,16,512]{4,3,1,0,2:T(8,128)S(1)} %copy.29), channel_id=1, replica_groups=mesh['pb'=4,'wa'=8] {'wa'}, dimensions={2} | all-to-all | bytes 4194304 | tf_op jit(solution)/shard_map/all_to_all | solution.py:31
  100.3 1.4 copy.48
  101.7 0.5 fusion.12
  102.2 0.3 copy.43
  102.5 0.3 copy.44
  102.9 1.0 fusion.4
  103.9 1.0 fusion.5
  104.9 1.0 convolution_add_fusion.2
  105.9 1.0 convolution_subtract_fusion.2
  106.9 0.7 stack.39
  107.7 1.3 copy.31
  108.9 0.7 stack.40
  110.8 1.0 fusion.8
  111.8 1.0 fusion.9
  112.7 1.0 convolution_add_fusion.1
  113.7 1.2 convolution_subtract_fusion.1
  115.1 0.7 copy.33
  116.0 0.7 copy.34
  116.7 0.6 maximum_bitcast_fusion.2
  117.2 0.5 fusion.10
  117.7 0.3 copy.45
  118.1 0.3 copy.46
  118.4 1.0 fusion.2
  119.4 1.0 fusion.3
  120.4 1.0 convolution_add_fusion
  121.5 1.0 convolution_subtract_fusion
  122.5 0.7 stack.45
  123.2 1.3 copy.35
  124.5 0.7 stack.46
  126.3 28.1 %all_to_all.22 = f32[2,4,8,16,512]{4,3,2,0,1:T(8,128)S(1)} all-to-all(f32[2,4,8,16,512]{4,3,2,0,1:T(8,128)S(1)} %copy.37), channel_id=1, replica_groups=mesh['pb'=4,'wa'=8] {'pb'}, dimensions={1} | all-to-all | bytes 4194304 | tf_op jit(solution)/shard_map/all_to_all | solution.py:32
  154.7 51.3 %all_to_all.23 = f32[2,4,8,16,512]{4,3,1,0,2:T(8,128)S(1)} all-to-all(f32[2,4,8,16,512]{4,3,1,0,2:T(8,128)S(1)} %copy.38), channel_id=1, replica_groups=mesh['pb'=4,'wa'=8] {'wa'}, dimensions={2} | all-to-all | bytes 4194304 | tf_op jit(solution)/shard_map/all_to_all | solution.py:31
  206.0 1.4 copy.40
  207.4 3.5 %reshape.72 = f32[2,262144]{1,0:T(2,128)} reshape(f32[2,4,2,16,4,512]{5,4,3,2,1,0:T(4,128)S(1)} %copy.40) | data formatting | bytes 4194304 | tf_op jit(solution)/shard_map/reshape | solution.py:48
  (21 shorter events, 3.6 us)
Async XLA Ops:
  1.5 6.8 %copy-start.3 = (f32[4,2,128,128]{3,2,1,0:T(8,128)S(1)}, f32[4,2,128,128]{3,2,1,0:T(8,128)}, u32[]{:S(2)}) copy-start(f32[4,2,128,128]{3,2,1,0:T(8,128)} %param.4) | copy-start | bytes 1572868
  14.3 1.2 copy-start
  108.9 1.2 copy-start.1
  124.5 1.2 copy-start.2
where the time goes:
time: 211 us
  blocking collectives  163 us (77%)
  local copies, waits for them, and re-layouts  27.2 us (13%)
  matrix products  16.4 us (8%)
  other arithmetic  4.25 us (2%)
    all_to_all x2, blocking collectives, trade_global(): lax.all_to_all(lax.all_to_all(packed, 'pb', split_axis=1, concat_axis=1,...  105 us
    all_to_all x2, blocking collectives, trade_global(): lax.all_to_all(packed, 'pb', split_axis=1, concat_axis=1, tiled=True)  57.9 us
    another operation x8, local copies, waits for them, and re-layouts, mix_left(): return jnp.stack([real, imag])  6.06 us
    slice x2, local copies, waits for them, and re-layouts, mix_right(): values[0]  4.46 us

commit v1 on v0

--- a/solution.py
+++ b/solution.py
@@ -4,6 +4,13 @@
 from jax.sharding import PartitionSpec as P
 
 HIGH = lax.Precision.HIGHEST
+
+
+def swap_blocks(block, name, split, join):
+    peers = lax.axis_size(name)
+    blocks = jnp.stack(jnp.split(block, peers, axis=split), axis=0)
+    blocks = lax.all_to_all(blocks, name, split_axis=0, concat_axis=0)
+    return jnp.concatenate(blocks, axis=join)
 
 
 def mix_left(gate, values):
@@ -28,12 +35,8 @@
 
 
 def trade_global(packed):
-    return lax.all_to_all(
-        lax.all_to_all(packed, "pb", split_axis=1, concat_axis=1, tiled=True),
-        "wa",
-        split_axis=2,
-        concat_axis=2,
-        tiled=True,
+    return swap_blocks(
+        lax.all_to_all(packed, "pb", split_axis=1, concat_axis=1, tiled=True), "wa", 2, 2
     )
 
 

time: 211 us -> 211 us (level)
  no operation moved by 1% of the time
where the time goes in v1:
time: 211 us
  blocking collectives  163 us (77%)
  local copies, waits for them, and re-layouts  27.2 us (13%)
  matrix products  16.4 us (8%)
  other arithmetic  4.25 us (2%)
    all_to_all x2, blocking collectives, swap_blocks(): blocks = lax.all_to_all(blocks, name, split_axis=0, concat_axis=0)  105 us
    all_to_all x2, blocking collectives, trade_global(): lax.all_to_all(packed, 'pb', split_axis=1, concat_axis=1, tiled=True)  57.9 us
    another operation x8, local copies, waits for them, and re-layouts, mix_left(): return jnp.stack([real, imag])  6.06 us
    slice x2, local copies, waits for them, and re-layouts, mix_right(): values[0]  4.46 us

profile of v1, /device:TPU:0, one launch (start us, length us, event | category | flops | bytes accessed | tf_op | source)
XLA Modules:
  0.0 211.0 jit_solution(6162761487790879801)
XLA Ops:
  0.0 1.5 fusion.30
  1.5 4.3 %fusion.29 = (f32[1,262144]{1,0:T(1,128)S(1)}, f32[1,262144]{1,0:T(1,128)S(1)}) fusion(f32[2,262144]{1,0:T(2,128)} %param.3), kind=kLoop, calls=%fused_computation.74 | loop fusion | bytes 4194304 | tf_op jit(solution)/shard_map/slice | solution.py:23
  5.7 1.3 iota_compare_fusion
  7.0 1.2 iota_compare_fusion.2
  8.5 1.0 fusion.22
  9.5 1.0 fusion.23
  10.5 1.0 fusion
  11.6 1.0 fusion.1
  12.6 0.3 copy.97
  12.9 1.3 stack.90
  14.6 0.4 stack.91
  15.0 0.5 copy-done
  15.5 0.5 maximum_bitcast_fusion
  16.0 0.7 copy.126
  16.7 29.7 %all_to_all.20 = f32[2,4,8,16,512]{4,3,2,0,1:T(8,128)S(1)} all-to-all(f32[2,4,8,16,512]{4,3,2,0,1:T(8,128)S(1)} %bitcast.201), channel_id=1, replica_groups=mesh['pb'=4,'wa'=8] {'pb'}, dimensions={1} | all-to-all | bytes 4194304 | tf_op jit(solution)/shard_map/all_to_all | solution.py:39
  46.6 53.6 %all_to_all.21 = f32[8,2,4,1,16,512]{5,4,1,2,3,0:T(8,128)S(1)} all-to-all(f32[8,2,4,1,16,512]{5,4,1,2,3,0:T(8,128)S(1)} %fusion.10), channel_id=1, replica_groups=mesh['pb'=4,'wa'=8] {'wa'}, dimensions={0} | all-to-all | bytes 4194304 | tf_op jit(solution)/shard_map/all_to_all | solution.py:12
  100.2 1.4 copy.147
  101.6 0.5 fusion.28
  102.1 0.3 copy.142
  102.4 0.3 copy.143
  102.8 1.0 fusion.20
  103.8 1.0 fusion.21
  104.8 1.0 convolution_add_fusion.2
  105.8 1.0 convolution_subtract_fusion.2
  106.8 0.7 stack.102
  107.6 1.3 copy.109
  108.9 0.7 stack.103
  110.7 1.0 fusion.24
  111.7 1.0 fusion.25
  112.7 1.0 convolution_add_fusion.1
  113.6 1.2 convolution_subtract_fusion.1
  115.0 0.7 copy.111
  115.9 0.7 copy.112
  116.6 0.6 maximum_bitcast_fusion.2
  117.1 0.5 fusion.26
  117.6 0.3 copy.144
  118.0 0.3 copy.145
  118.3 1.0 fusion.18
  119.3 1.0 fusion.19
  120.3 1.0 convolution_add_fusion
  121.4 1.0 convolution_subtract_fusion
  122.4 0.7 stack.108
  123.1 1.3 copy.113
  124.4 0.7 stack.109
  126.2 28.1 %all_to_all.22 = f32[2,4,8,16,512]{4,3,2,0,1:T(8,128)S(1)} all-to-all(f32[2,4,8,16,512]{4,3,2,0,1:T(8,128)S(1)} %copy.115), channel_id=1, replica_groups=mesh['pb'=4,'wa'=8] {'pb'}, dimensions={1} | all-to-all | bytes 4194304 | tf_op jit(solution)/shard_map/all_to_all | solution.py:39
  154.8 51.3 %all_to_all.23 = f32[8,2,4,1,16,512]{5,4,2,1,3,0:T(8,128)S(1)} all-to-all(f32[8,2,4,1,16,512]{5,4,2,1,3,0:T(8,128)S(1)} %copy.123), channel_id=1, replica_groups=mesh['pb'=4,'wa'=8] {'wa'}, dimensions={0} | all-to-all | bytes 4194304 | tf_op jit(solution)/shard_map/all_to_all | solution.py:12
  206.1 1.4 copy.125
  207.5 3.5 %reshape.72 = f32[2,262144]{1,0:T(2,128)} reshape(f32[2,4,2,16,4,512]{5,4,3,2,1,0:T(4,128)S(1)} %copy.125) | data formatting | bytes 4194304 | tf_op jit(solution)/shard_map/reshape | solution.py:51
  (36 shorter events, 3.6 us)
Async XLA Ops:
  1.5 6.8 %copy-start.3 = (f32[4,2,128,128]{3,2,1,0:T(8,128)S(1)}, f32[4,2,128,128]{3,2,1,0:T(8,128)}, u32[]{:S(2)}) copy-start(f32[4,2,128,128]{3,2,1,0:T(8,128)} %param.4) | copy-start | bytes 1572868
  14.3 1.2 copy-start
  108.9 1.2 copy-start.1
  124.4 1.2 copy-start.2
